TPU v7x, 32 devices: a whole 2x2x4 slice. The times are simulated.
32 devices in a mesh: box: 8 (over z, x), dir: 4 (over y, core).
Axes of the slice: x: 2, y: 2, z: 4, core: 2. Of those that a mesh axis runs over, the one named last changes fastest.
Arguments:
- leaf_patterns: float32 [16, 16, 2, 64, 128], P('box', 'dir'), may hold values from -6 to 6
- occupancy: int32 [16], P('box'), may hold values from 0 to 16
- pair_lists: int32 [4, 1, 4], replicated, may hold values from 0 to 2, as said below
Outputs:
- translated: float32 [8, 1, 16, 2, 128, 512], P('box', None, None, None, 'dir')
Inputs may be any that keep to these rules, and one draw needn't show every extreme that they name: `pair_lists`: each box's list names 4 source boxes, repeats allowed: positions 0 to 0 are the boxes of the pair before its own, 1 to 1 its own pair, the rest the pair after; never the box itself and never a pair outside 0 .. 3.
All inputs are finite; a program needn't handle non-finite values.
Results may differ from a plain program's by a relative error of at most 0.0003.
Values sent between devices are 32-bit elements; how exact they have to be, the bound alone decides.
A program may use at most 64 MiB of HBM per device.

v0:
```python
import functools

import jax
import jax.numpy as jnp
import numpy as np
from jax import lax
from jax.experimental import pallas as pl
from jax.experimental.pallas import tpu as pltpu
from jax.sharding import PartitionSpec as P

MESH = pl.DeviceIdType.MESH
LTR = 16
full_count = 16.0
phase_first = 16.0
phase_second = 64.0
translate_wave = 20.0


def interp_table(points, offset):
    orders = np.arange(points // 2 + 1, dtype=np.float64)
    weights = np.where((orders == 0) | (orders == points // 2), 1.0, 2.0) / points
    source = (np.arange(points) + offset) / points
    target = (np.arange(2 * points) + offset) / (2 * points)
    angle = 2.0 * np.pi * (target[:, None, None] - source[None, :, None]) * orders
    return (np.cos(angle) * weights).sum(-1)


def halves(table):
    high = np.asarray(table, np.float32).astype(jnp.bfloat16)
    low = (np.asarray(table, np.float64) - high.astype(np.float64)).astype(jnp.bfloat16)
    return high, low


def sines(rows, columns):
    theta = np.pi * (np.arange(rows) + 0.5) / rows
    phi = 2.0 * np.pi * np.arange(columns) / columns
    return np.sin(theta), np.cos(theta), np.cos(phi), np.sin(phi)


def center(g):
    return np.array([g % 4, g // 4 % 4, g // 16], np.float64)


def series_table(pairs):
    table = np.zeros((pairs, 2 * (3 + 2 * (LTR + 1))), np.float64)
    width = 3 + 2 * (LTR + 1)
    for g in range(pairs):
        for side, s in enumerate((g - 1, g + 1)):
            if not 0 <= s < pairs:
                continue
            r = center(g) - center(s)
            distance = np.sqrt((r * r).sum())
            x = translate_wave * distance
            now = (np.sin(x) - 1j * np.cos(x)) / x
            nxt = ((np.sin(x) - x * np.cos(x)) - 1j * (x * np.sin(x) + np.cos(x))) / x**2
            table[g, side * width : side * width + 3] = r / distance
            for degree in range(LTR + 1):
                value = (1j**degree) * (2 * degree + 1) * now
                table[g, side * width + 3 + 2 * degree] = value.real
                table[g, side * width + 4 + 2 * degree] = value.imag
                now, nxt = nxt, (2 * degree + 3) / x * nxt - now
    return table.astype(np.float32)


def split(value):
    high = value.astype(jnp.bfloat16)
    low = (value - high.astype(jnp.float32)).astype(jnp.bfloat16)
    return high, low


def dot(a, b):
    return jnp.dot(a, b, preferred_element_type=jnp.float32)


def kernel(
    sizes,
    leaf, occ, lists, series, c1, r1, r2, c2, ph1, ph2, polar, azim,
    out,
    mine, other, lhs1, rhs1, first, rhs2, lhs2, ready, relay, land, oper,
    xs, xr, ds, dr, zs, zr,
):
    n_box, n_dir, count, lt, lp, slab = sizes
    box = lax.axis_index("box")
    me = lax.axis_index("dir")
    half = box % 2
    pair = box // 2
    pairs = n_box // 2
    has_lower = pair > 0
    has_upper = pair < pairs - 1
    partner = box + 1 - 2 * half

    barrier = pltpu.get_barrier_semaphore()
    pl.semaphore_signal(barrier, inc=1, device_id=(partner, me), device_id_type=MESH)
    for o in range(1, n_dir):
        pl.semaphore_signal(
            barrier, inc=1, device_id=(box, (me + o) % n_dir), device_id_type=MESH
        )

    @pl.when(has_lower)
    def _():
        pl.semaphore_signal(barrier, inc=1, device_id=(box - 2, me), device_id_type=MESH)

    @pl.when(has_upper)
    def _():
        pl.semaphore_signal(barrier, inc=1, device_id=(box + 2, me), device_id_type=MESH)

    w0 = occ[0].astype(jnp.float32) / full_count
    w1 = occ[1].astype(jnp.float32) / full_count
    for r in range(count):
        for c in range(2):
            a = leaf[0, r, c] * w0
            b = leaf[1, r, c] * w1
            mine[r, c] = a + b
            mine[r, 2 + c] = b - a

    pl.semaphore_wait(
        barrier, n_dir + has_lower.astype(jnp.int32) + has_upper.astype(jnp.int32)
    )

    def x_copy(r):
        return pltpu.make_async_remote_copy(
            mine.at[r], other.at[r], xs.at[r], xr.at[r], (partner, me), device_id_type=MESH
        )

    for r in range(count):
        x_copy(r).start()

    def d_copy(r, o):
        peer = (me + o) % n_dir
        return pltpu.make_async_remote_copy(
            ready.at[r, peer], relay.at[me, r], ds.at[r, o], dr.at[r, n_dir - o],
            (box, peer), device_id_type=MESH,
        )

    def d_arrival(r, o):
        peer = (me + o) % n_dir
        return pltpu.make_async_remote_copy(
            ready.at[r, me], relay.at[peer, r], ds.at[r, o], dr.at[r, o],
            (box, peer), device_id_type=MESH,
        )

    def z_copy(r, o, up):
        source = (me + o) % n_dir
        chunk = ready.at[r, me] if o == 0 else relay.at[source, r]
        side = 0 if up else 1
        return pltpu.make_async_remote_copy(
            chunk, land.at[side, source, r], zs.at[side, r, o], zr.at[side, r, o],
            (box + 2 if up else box - 2, me), device_id_type=MESH,
        )

    def z_start(r, o):
        @pl.when(has_upper)
        def _():
            z_copy(r, o, True).start()

        @pl.when(has_lower)
        def _():
            z_copy(r, o, False).start()

    for side, present in ((0, has_lower), (1, has_upper)):
        @pl.when(jnp.logical_not(present))
        def _():
            land[side] = jnp.zeros(land.shape[1:], jnp.float32)

    def first_level(source, r):
        for k in range(4):
            high, low = split(source[r, k])
            rows = pl.ds(k * lt, lt)
            lhs1[rows, 0:lp] = high
            lhs1[rows, lp : 2 * lp] = low
            lhs1[rows, 2 * lp : 3 * lp] = high
        wide = dot(lhs1[...], c1[...])
        for k in range(4):
            high, low = split(wide[k * lt : (k + 1) * lt])
            columns = pl.ds(k * 2 * lp, 2 * lp)
            rhs1[0:lt, columns] = high
            rhs1[lt : 2 * lt, columns] = low
            rhs1[2 * lt : 3 * lt, columns] = high
        sr, si, dre, dim = [
            dot(r1[...], rhs1[:, k * 2 * lp : (k + 1) * 2 * lp]) for k in range(4)
        ]
        cosine, sine = ph1[0], ph1[1]
        return cosine * sr - sine * dim, cosine * si + sine * dre

    sign = (2 * half - 1).astype(jnp.float32)
    row_start = pl.multiple_of(half * 2 * lt, 2 * lt)

    def level_step(r, carry):
        fr, fi = first_level(mine, r)
        first[0] = fr
        first[1] = fi
        x_copy(r).wait_recv()
        gr, gi = first_level(other, r)
        for k, value in enumerate(
            (first[0] + gr, first[1] + gi, (first[0] - gr) * sign, (first[1] - gi) * sign)
        ):
            high, low = split(value)
            columns = pl.ds(k * 2 * lp, 2 * lp)
            rhs2[0 : 2 * lt, columns] = high
            rhs2[2 * lt : 4 * lt, columns] = low
            rhs2[4 * lt : 6 * lt, columns] = high
        for k in range(4):
            high, low = split(dot(r2[half], rhs2[:, k * 2 * lp : (k + 1) * 2 * lp]))
            rows = pl.ds(k * 2 * lt, 2 * lt)
            lhs2[rows, 0 : 2 * lp] = high
            lhs2[rows, 2 * lp : 4 * lp] = low
            lhs2[rows, 4 * lp : 6 * lp] = high
        for d in range(n_dir):
            sr, si, dre, dim = [
                dot(lhs2[pl.ds(k * 2 * lt + d * slab, slab), :], c2[...]) for k in range(4)
            ]
            rows = pl.ds(row_start + d * slab, slab)
            cosine, sine = ph2[0, rows], ph2[1, rows]
            ready[r, d, 0] = cosine * sr - sine * dim
            ready[r, d, 1] = cosine * si + sine * dre
        z_start(r, 0)
        for o in range(1, n_dir):
            d_copy(r, o).start()

        @pl.when(r > 0)
        def _():
            for o in range(1, n_dir):
                d_arrival(r - 1, o).wait_recv()
                z_start(r - 1, o)

        return carry

    lax.fori_loop(0, count, level_step, 0)
    for o in range(1, n_dir):
        d_arrival(count - 1, o).wait_recv()
        z_start(count - 1, o)

    slots = lists.shape[1]
    entries = lists.shape[2]
    slab_rows = pl.ds(pl.multiple_of(half * 2 * lt + me * slab, slab), slab)
    sine_theta = polar[0, slab_rows]
    along_x = sine_theta * azim[0:1]
    along_y = sine_theta * azim[1:2]
    along_z = polar[1, slab_rows] * jnp.ones_like(along_x)
    width = 3 + 2 * (LTR + 1)
    for side in range(2):
        named = jnp.float32(0.0)
        for k in range(entries):
            chosen = lists[pair, 0, k]
            hit = chosen < slots if side == 0 else chosen >= 2 * slots
            named = named + jnp.where(hit, 1.0, 0.0)
        scale = named / entries
        base = side * width
        u = (
            series[pair, base] * along_x
            + series[pair, base + 1] * along_y
            + series[pair, base + 2] * along_z
        )
        now, nxt = jnp.ones_like(u), u
        real, imag = jnp.zeros_like(u), jnp.zeros_like(u)
        for degree in range(LTR + 1):
            real = real + series[pair, base + 3 + 2 * degree] * now
            imag = imag + series[pair, base + 4 + 2 * degree] * now
            now, nxt = nxt, (
                ((2.0 * degree + 3.0) / (degree + 2.0)) * (u * nxt)
                - ((degree + 1.0) / (degree + 2.0)) * now
            )
        oper[side, 0] = real * scale
        oper[side, 1] = imag * scale

    def apply_step(r, carry):
        for o in range(n_dir):
            source = (me + o) % n_dir

            @pl.when(has_lower)
            def _():
                z_copy(r, o, True).wait_recv()

            @pl.when(has_upper)
            def _():
                z_copy(r, o, False).wait_recv()

            lr, li = land[0, source, r, 0], land[0, source, r, 1]
            ur, ui = land[1, source, r, 0], land[1, source, r, 1]
            out[source, r, 0] = (
                oper[0, 0] * lr - oper[0, 1] * li + oper[1, 0] * ur - oper[1, 1] * ui
            )
            out[source, r, 1] = (
                oper[0, 0] * li + oper[0, 1] * lr + oper[1, 0] * ui + oper[1, 1] * ur
            )
        return carry

    lax.fori_loop(0, count, apply_step, 0)

    for r in range(count):
        x_copy(r).wait_send()
        for o in range(1, n_dir):
            d_copy(r, o).wait_send()
        for o in range(n_dir):
            @pl.when(has_upper)
            def _():
                z_copy(r, o, True).wait_send()

            @pl.when(has_lower)
            def _():
                z_copy(r, o, False).wait_send()


def per_device(n_box, n_dir, leaf_patterns, occupancy, pair_lists):
    _, count, _, lt, lp = leaf_patterns.shape
    assert leaf_patterns.shape[0] == 2
    slab = 2 * lt // n_dir
    bf16 = jnp.bfloat16
    first_high, first_low = halves(interp_table(lp, 0.0).T)
    c1 = np.concatenate([first_high, first_high, first_low], axis=0)
    row_high, row_low = halves(interp_table(lt, 0.5))
    r1 = np.concatenate([row_high, row_high, row_low], axis=1)
    row_high, row_low = halves(interp_table(2 * lt, 0.5).reshape(2, 2 * lt, 2 * lt))
    r2 = np.concatenate([row_high, row_high, row_low], axis=2)
    high, low = halves(interp_table(2 * lp, 0.0).T)
    c2 = np.concatenate([high, high, low], axis=0)
    st, _, cp, _ = sines(2 * lt, 2 * lp)
    angle = phase_first * st[:, None] * cp[None]
    ph1 = np.stack([np.cos(angle), np.sin(angle)]).astype(np.float32)
    st, ct, cp, sp = sines(4 * lt, 4 * lp)
    angle = phase_second * st[:, None] * sp[None]
    ph2 = np.stack([np.cos(angle), np.sin(angle)]).astype(np.float32)
    polar = np.stack([st, ct])[:, :, None].astype(np.float32)
    azim = np.stack([cp, sp]).astype(np.float32)
    series = series_table(n_box // 2)
    vmem = pl.BlockSpec(memory_space=pltpu.VMEM)
    smem = pl.BlockSpec(memory_space=pltpu.SMEM)
    chunk = (2, slab, 4 * lp)
    f32 = jnp.float32
    result = pl.pallas_call(
        functools.partial(kernel, (n_box, n_dir, count, lt, lp, slab)),
        out_shape=jax.ShapeDtypeStruct((n_dir, count) + chunk, f32),
        in_specs=[vmem, smem, smem, smem] + [vmem] * 8,
        out_specs=vmem,
        scratch_shapes=[
            pltpu.VMEM((count, 4, lt, lp), f32),
            pltpu.VMEM((count, 4, lt, lp), f32),
            pltpu.VMEM((4 * lt, 3 * lp), bf16),
            pltpu.VMEM((3 * lt, 8 * lp), bf16),
            pltpu.VMEM((2, 2 * lt, 2 * lp), f32),
            pltpu.VMEM((6 * lt, 8 * lp), bf16),
            pltpu.VMEM((8 * lt, 6 * lp), bf16),
            pltpu.VMEM((count, n_dir) + chunk, f32),
            pltpu.VMEM((n_dir, count) + chunk, f32),
            pltpu.VMEM((2, n_dir, count) + chunk, f32),
            pltpu.VMEM((2,) + chunk, f32),
            pltpu.SemaphoreType.DMA((count,)),
            pltpu.SemaphoreType.DMA((count,)),
            pltpu.SemaphoreType.DMA((count, n_dir)),
            pltpu.SemaphoreType.DMA((count, n_dir)),
            pltpu.SemaphoreType.DMA((2, count, n_dir)),
            pltpu.SemaphoreType.DMA((2, count, n_dir)),
        ],
        compiler_params=pltpu.CompilerParams(
            collective_id=0, has_side_effects=True, vmem_limit_bytes=48 << 20
        ),
    )(
        leaf_patterns, occupancy, pair_lists, jnp.asarray(series), jnp.asarray(c1),
        jnp.asarray(r1), jnp.asarray(r2), jnp.asarray(c2), jnp.asarray(ph1),
        jnp.asarray(ph2), jnp.asarray(polar), jnp.asarray(azim),
    )
    return result.reshape(1, 1, n_dir * count, *chunk)


def solution(mesh):
    placed = (P("box", "dir", None, None, None), P("box"), P())
    return jax.shard_map(
        functools.partial(per_device, mesh.shape["box"], mesh.shape["dir"]),
        mesh=mesh,
        in_specs=placed,
        out_specs=P("box", None, None, None, "dir", None),
        check_vma=False,
    )
```

profile of v0, /device:TPU:1, one launch (start us, length us, event | category | flops | bytes accessed | tf_op | source)
XLA Modules:
  0.0 72.2 jit_solution(15310635039360693171)
XLA Ops:
  0.0 0.0 copy-start
  0.0 1.2 %copy-done = f32[2,256,512]{2,1,0:T(8,128)S(1)} copy-done((f32[2,256,512]{2,1,0:T(8,128)S(1)}, f32[2,256,512]{2,1,0:T(8,128)}, u32[]{:S(2)}) %copy-start) | copy-done | bytes 1048600
  1.2 0.0 copy-start.1
  1.2 1.1 %copy-done.1 = bf16[768,512]{1,0:T(8,128)(2,1)S(1)} copy-done((bf16[768,512]{1,0:T(8,128)(2,1)S(1)}, bf16[768,512]{1,0:T(8,128)(2,1)}, u32[]{:S(2)}) %copy-start.1) | copy-done | bytes 786456
  2.4 0.0 copy-start.2
  2.4 1.0 %copy-done.2 = f32[2,4,2,64,128]{4,3,2,1,0:T(8,128)S(1)} copy-done((f32[2,4,2,64,128]{4,3,2,1,0:T(8,128)S(1)}, f32[2,4,2,64,128]{4,3,2,1,0:T(8,128)}, u32[]{:S(2)}) %copy-start.2) | copy-done | bytes 524312
  3.4 0.0 copy-start.3
  3.4 0.9 %copy-done.3 = f32[2,256,1]{2,1,0:T(8,128)S(1)} copy-done((f32[2,256,1]{2,1,0:T(8,128)S(1)}, f32[2,256,1]{2,1,0:T(8,128)}, u32[]{:S(2)}) %copy-start.3) | copy-done | bytes 2072
  4.4 0.0 copy-start.4
  4.4 0.9 %copy-done.4 = f32[2,128,256]{2,1,0:T(8,128)S(1)} copy-done((f32[2,128,256]{2,1,0:T(8,128)S(1)}, f32[2,128,256]{2,1,0:T(8,128)}, u32[]{:S(2)}) %copy-start.4) | copy-done | bytes 262168
  5.3 0.0 copy-start.5
  5.3 0.9 %copy-done.5 = bf16[2,128,384]{2,1,0:T(8,128)(2,1)S(1)} copy-done((bf16[2,128,384]{2,1,0:T(8,128)(2,1)S(1)}, bf16[2,128,384]{2,1,0:T(8,128)(2,1)}, u32[]{:S(2)}) %copy-start.5) | copy-done | bytes 196632
  6.2 0.0 copy-start.6
  6.2 0.9 %copy-done.6 = bf16[384,256]{1,0:T(8,128)(2,1)S(1)} copy-done((bf16[384,256]{1,0:T(8,128)(2,1)S(1)}, bf16[384,256]{1,0:T(8,128)(2,1)}, u32[]{:S(2)}) %copy-start.6) | copy-done | bytes 196632
  7.2 0.0 copy-start.7
  7.2 0.8 %copy-done.7 = bf16[128,192]{1,0:T(8,128)(2,1)S(1)} copy-done((bf16[128,192]{1,0:T(8,128)(2,1)S(1)}, bf16[128,192]{1,0:T(8,128)(2,1)}, u32[]{:S(2)}) %copy-start.7) | copy-done | bytes 49176
  8.0 0.0 copy-start.8
  8.0 0.7 copy-done.8
  8.7 0.0 copy-start.9
  8.7 0.7 copy-done.9
  9.4 0.0 copy-start.10
  9.4 0.7 copy-done.10
  10.0 0.0 copy-start.11
  10.1 0.7 copy-done.11
  10.7 60.2 %shard_map.118 = f32[4,4,2,32,512]{4,3,2,1,0:T(8,128)S(1)} custom-call(f32[2,4,2,64,128]{4,3,2,1,0:T(8,128)S(1)} %copy-done.2, s32[2]{0:T(128)S(1)} %copy-done.11, s32[4,1,4]{2,1,0:T(1,128)S(1)} %copy-done.9, f32[4,74]{1,0:T(4,128)S(1)} %copy-done.10, bf16[384,256]{1,0:T(8,128)(2,1)S(1)} %copy-done.6, bf16[128,192]{1,0:T(8,128)(2,1)S(1)} %copy-done.7, ...), custom_call_target="tpu_custom_call" | custom-call | tf_op jit(solution)/shard_map/pallas_call | solution.py:330
  70.9 1.3 %copy.14 = f32[1,1,16,2,32,512]{5,4,3,2,1,0:T(8,128)} copy(f32[1,1,16,2,32,512]{5,4,3,2,1,0:T(8,128)S(1)} %bitcast.1) | data formatting | bytes 4194304
Async XLA Ops:
  0.0 1.2 %copy-start = (f32[2,256,512]{2,1,0:T(8,128)S(1)}, f32[2,256,512]{2,1,0:T(8,128)}, u32[]{:S(2)}) copy-start(f32[2,256,512]{2,1,0:T(8,128)} %constant.24.clone.ph2) | copy-start | bytes 3145732
  1.2 1.1 %copy-start.1 = (bf16[768,512]{1,0:T(8,128)(2,1)S(1)}, bf16[768,512]{1,0:T(8,128)(2,1)}, u32[]{:S(2)}) copy-start(bf16[768,512]{1,0:T(8,128)(2,1)} %constant.22.clone.c2) | copy-start | bytes 2359300
  2.4 1.0 %copy-start.2 = (f32[2,4,2,64,128]{4,3,2,1,0:T(8,128)S(1)}, f32[2,4,2,64,128]{4,3,2,1,0:T(8,128)}, u32[]{:S(2)}) copy-start(f32[2,4,2,64,128]{4,3,2,1,0:T(8,128)} %leaf.1) | copy-start | bytes 1572868
  3.4 0.9 %copy-start.3 = (f32[2,256,1]{2,1,0:T(8,128)S(1)}, f32[2,256,1]{2,1,0:T(8,128)}, u32[]{:S(2)}) copy-start(f32[2,256,1]{2,1,0:T(8,128)} %constant.25.clone.polar) | copy-start | bytes 6148
  4.4 0.9 %copy-start.4 = (f32[2,128,256]{2,1,0:T(8,128)S(1)}, f32[2,128,256]{2,1,0:T(8,128)}, u32[]{:S(2)}) copy-start(f32[2,128,256]{2,1,0:T(8,128)} %constant.23.clone.ph1) | copy-start | bytes 786436
  5.3 0.9 %copy-start.5 = (bf16[2,128,384]{2,1,0:T(8,128)(2,1)S(1)}, bf16[2,128,384]{2,1,0:T(8,128)(2,1)}, u32[]{:S(2)}) copy-start(bf16[2,128,384]{2,1,0:T(8,128)(2,1)} %constant.21.clone.r2) | copy-start | bytes 589828
  6.2 0.9 %copy-start.6 = (bf16[384,256]{1,0:T(8,128)(2,1)S(1)}, bf16[384,256]{1,0:T(8,128)(2,1)}, u32[]{:S(2)}) copy-start(bf16[384,256]{1,0:T(8,128)(2,1)} %constant.19.clone.c1) | copy-start | bytes 589828
  7.2 0.8 %copy-start.7 = (bf16[128,192]{1,0:T(8,128)(2,1)S(1)}, bf16[128,192]{1,0:T(8,128)(2,1)}, u32[]{:S(2)}) copy-start(bf16[128,192]{1,0:T(8,128)(2,1)} %constant.20.clone.r1) | copy-start | bytes 147460
  8.0 0.7 copy-start.8
  8.7 0.7 copy-start.9
  9.4 0.7 copy-start.10
  10.0 0.7 copy-start.11
where the time goes:
time: 72.7 us; the launch traced here: 72.2 us
  Pallas kernels  60.2 us (83%)
  local copies, waits for them, and re-layouts  12 us (17%)
    pallas_call x1, Pallas kernels, per_device(): pl.pallas_call(functools.partial(kernel, (n_box, n_dir, count, lt, lp, sl...  60.2 us
    unnamed x25, local copies, waits for them, and re-layouts  12 us

commit v1 on v0

v1 whole, which is shorter than its diff:
```python
import functools

import jax
import jax.numpy as jnp
import numpy as np
from jax import lax
from jax.experimental import pallas as pl
from jax.experimental.pallas import tpu as pltpu
from jax.sharding import PartitionSpec as P

MESH = pl.DeviceIdType.MESH
LTR = 16
full_count = 16.0
phase_first = 16.0
phase_second = 64.0
translate_wave = 20.0


def interp_table(points, offset):
    orders = np.arange(points // 2 + 1, dtype=np.float64)
    weights = np.where((orders == 0) | (orders == points // 2), 1.0, 2.0) / points
    source = (np.arange(points) + offset) / points
    target = (np.arange(2 * points) + offset) / (2 * points)
    angle = 2.0 * np.pi * (target[:, None, None] - source[None, :, None]) * orders
    return (np.cos(angle) * weights).sum(-1)


def halves(table):
    high = np.asarray(table, np.float32).astype(jnp.bfloat16)
    low = (np.asarray(table, np.float64) - high.astype(np.float64)).astype(jnp.bfloat16)
    return high, low


def sines(rows, columns):
    theta = np.pi * (np.arange(rows) + 0.5) / rows
    phi = 2.0 * np.pi * np.arange(columns) / columns
    return np.sin(theta), np.cos(theta), np.cos(phi), np.sin(phi)


def center(g):
    return np.array([g % 4, g // 4 % 4, g // 16], np.float64)


def series_table(pairs):
    table = np.zeros((pairs, 2 * (3 + 2 * (LTR + 1))), np.float64)
    width = 3 + 2 * (LTR + 1)
    for g in range(pairs):
        for side, s in enumerate((g - 1, g + 1)):
            if not 0 <= s < pairs:
                continue
            r = center(g) - center(s)
            distance = np.sqrt((r * r).sum())
            x = translate_wave * distance
            now = (np.sin(x) - 1j * np.cos(x)) / x
            nxt = ((np.sin(x) - x * np.cos(x)) - 1j * (x * np.sin(x) + np.cos(x))) / x**2
            table[g, side * width : side * width + 3] = r / distance
            for degree in range(LTR + 1):
                value = (1j**degree) * (2 * degree + 1) * now
                table[g, side * width + 3 + 2 * degree] = value.real
                table[g, side * width + 4 + 2 * degree] = value.imag
                now, nxt = nxt, (2 * degree + 3) / x * nxt - now
    return table.astype(np.float32)


def split(value):
    high = value.astype(jnp.bfloat16)
    low = (value - high.astype(jnp.float32)).astype(jnp.bfloat16)
    return high, low


def dot(a, b):
    return jnp.dot(a, b, preferred_element_type=jnp.float32)


def kernel(
    sizes,
    leaf_in, occ_in, lists_in, series_in, c1_in, r1_in, r2_in, c2_in, ph1_in, ph2_in,
    polar_in, azim_in,
    out,
    leaf, occ, lists, series, c1, r1, r2, c2, ph1, ph2, polar, azim,
    mine, taken, lhs1, rhs1, first, rhs2, lhs2, ready, oper,
    loads, ls, lr, ds, dr,
):
    n_box, n_dir, count, lt, lp, slab = sizes
    box = lax.axis_index("box")
    me = lax.axis_index("dir")
    half = box % 2
    pair = box // 2
    has_lower = pair > 0
    has_upper = pair < n_box // 2 - 1
    partner = box + 1 - 2 * half
    row_start = pl.multiple_of(half * 2 * lt, 2 * lt)

    barrier = pltpu.get_barrier_semaphore()
    for o in range(1, n_dir):
        pl.semaphore_signal(
            barrier, inc=1, device_id=(box, (me + o) % n_dir), device_id_type=MESH
        )
    for present, by in ((has_lower, -2), (has_upper, 2)):
        @pl.when(present)
        def _():
            for start in (box, partner):
                pl.semaphore_signal(
                    barrier, inc=1, device_id=(start + by, me), device_id_type=MESH
                )

    half_rows = pl.ds(row_start, 2 * lt)
    pairs_in = (
        (leaf_in, leaf), (occ_in, occ), (lists_in, lists), (series_in, series),
        (polar_in.at[:, half_rows], polar), (azim_in, azim), (c1_in, c1), (r1_in, r1),
        (ph1_in, ph1), (r2_in.at[half], r2), (c2_in, c2), (ph2_in.at[:, half_rows], ph2),
    )
    copies = [
        pltpu.make_async_copy(source, target, loads.at[i])
        for i, (source, target) in enumerate(pairs_in)
    ]
    for copy in copies:
        copy.start()
    copies[1].wait()
    copies[0].wait()

    w0 = occ[0].astype(jnp.float32) / full_count
    w1 = occ[1].astype(jnp.float32) / full_count
    for r in range(count):
        for c in range(2):
            a = leaf[0, r, c] * w0
            b = leaf[1, r, c] * w1
            mine[r, c] = a + b
            mine[r, 2 + c] = b - a

    pl.semaphore_wait(
        barrier,
        n_dir - 1 + 2 * has_lower.astype(jnp.int32) + 2 * has_upper.astype(jnp.int32),
    )

    def l_copy(r, side, place):
        target = (box if place == 0 else partner) + 2 - 4 * side
        return pltpu.make_async_remote_copy(
            mine.at[r], taken.at[side, r, place], ls.at[side, r, place],
            lr.at[side, r, place], (target, me), device_id_type=MESH,
        )

    for r in range(count):
        for place in range(2):
            @pl.when(has_upper)
            def _():
                l_copy(r, 0, place).start()

            @pl.when(has_lower)
            def _():
                l_copy(r, 1, place).start()

    def d_copy(r, o):
        peer = (me + o) % n_dir
        return pltpu.make_async_remote_copy(
            ready.at[r, peer], out.at[me, r], ds.at[r, o], dr.at[r, n_dir - o],
            (box, peer), device_id_type=MESH,
        )

    def d_arrival(r, o):
        peer = (me + o) % n_dir
        return pltpu.make_async_remote_copy(
            ready.at[r, me], out.at[peer, r], ds.at[r, o], dr.at[r, o],
            (box, peer), device_id_type=MESH,
        )

    ready[...] = jnp.zeros(ready.shape, jnp.float32)
    for copy in copies[2:6]:
        copy.wait()

    slots = lists.shape[1]
    entries = lists.shape[2]
    width = 3 + 2 * (LTR + 1)
    for side in range(2):
        named = jnp.float32(0.0)
        for k in range(entries):
            chosen = lists[pair, 0, k]
            hit = chosen < slots if side == 0 else chosen >= 2 * slots
            named = named + jnp.where(hit, 1.0, 0.0)
        scale = named / entries
        base = side * width

        def oper_step(i, carry):
            rows = pl.ds(pl.multiple_of(i * 8, 8), 8)
            along_x = polar[0, rows] * azim[0:1]
            along_y = polar[0, rows] * azim[1:2]
            along_z = polar[1, rows] * jnp.ones_like(along_x)
            u = (
                series[pair, base] * along_x
                + series[pair, base + 1] * along_y
                + series[pair, base + 2] * along_z
            )
            now, nxt = jnp.ones_like(u), u
            real, imag = jnp.zeros_like(u), jnp.zeros_like(u)
            for degree in range(LTR + 1):
                real = real + series[pair, base + 3 + 2 * degree] * now
                imag = imag + series[pair, base + 4 + 2 * degree] * now
                now, nxt = nxt, (
                    ((2.0 * degree + 3.0) / (degree + 2.0)) * (u * nxt)
                    - ((degree + 1.0) / (degree + 2.0)) * now
                )
            oper[side, 0, rows] = real * scale
            oper[side, 1, rows] = imag * scale
            return carry

        lax.fori_loop(0, 2 * lt // 8, oper_step, 0)

    for copy in copies[6:]:
        copy.wait()

    def first_level(source):
        for k in range(4):
            high, low = split(source[k])
            rows = pl.ds(k * lt, lt)
            lhs1[rows, 0:lp] = high
            lhs1[rows, lp : 2 * lp] = low
            lhs1[rows, 2 * lp : 3 * lp] = high
        wide = dot(lhs1[...], c1[...])
        for k in range(4):
            high, low = split(wide[k * lt : (k + 1) * lt])
            columns = pl.ds(k * 2 * lp, 2 * lp)
            rhs1[0:lt, columns] = high
            rhs1[lt : 2 * lt, columns] = low
            rhs1[2 * lt : 3 * lt, columns] = high
        sr, si, dre, dim = [
            dot(r1[...], rhs1[:, k * 2 * lp : (k + 1) * 2 * lp]) for k in range(4)
        ]
        cosine, sine = ph1[0], ph1[1]
        return cosine * sr - sine * dim, cosine * si + sine * dre

    sign = (2 * half - 1).astype(jnp.float32)

    def add_side(r, side):
        for place in range(2):
            l_copy(r, side, place).wait_recv()
            fr, fi = first_level(taken.at[side, r, place])
            if place == 0:
                first[0] = fr
                first[1] = fi
        for k, value in enumerate(
            (first[0] + fr, first[1] + fi, (first[0] - fr) * sign, (first[1] - fi) * sign)
        ):
            high, low = split(value)
            columns = pl.ds(k * 2 * lp, 2 * lp)
            rhs2[0 : 2 * lt, columns] = high
            rhs2[2 * lt : 4 * lt, columns] = low
            rhs2[4 * lt : 6 * lt, columns] = high
        for k in range(4):
            high, low = split(dot(r2[...], rhs2[:, k * 2 * lp : (k + 1) * 2 * lp]))
            rows = pl.ds(k * 2 * lt, 2 * lt)
            lhs2[rows, 0 : 2 * lp] = high
            lhs2[rows, 2 * lp : 4 * lp] = low
            lhs2[rows, 4 * lp : 6 * lp] = high
        for d in range(n_dir):
            sr, si, dre, dim = [
                dot(lhs2[pl.ds(k * 2 * lt + d * slab, slab), :], c2[...]) for k in range(4)
            ]
            rows = pl.ds(d * slab, slab)
            cosine, sine = ph2[0, rows], ph2[1, rows]
            gr = cosine * sr - sine * dim
            gi = cosine * si + sine * dre
            pr, pi = oper[side, 0, rows], oper[side, 1, rows]
            ready[r, d, 0] += pr * gr - pi * gi
            ready[r, d, 1] += pr * gi + pi * gr

    def level_step(q, carry):
        r = q // 2
        side = q % 2

        @pl.when(jnp.where(side == 0, has_lower, has_upper))
        def _():
            add_side(r, side)

        @pl.when(side == 1)
        def _():
            for o in range(1, n_dir):
                d_copy(r, o).start()
            out[me, r] = ready[r, me]

        return carry

    lax.fori_loop(0, 2 * count, level_step, 0)

    for r in range(count):
        for o in range(1, n_dir):
            d_arrival(r, o).wait_recv()
            d_copy(r, o).wait_send()
        for place in range(2):
            @pl.when(has_upper)
            def _():
                l_copy(r, 0, place).wait_send()

            @pl.when(has_lower)
            def _():
                l_copy(r, 1, place).wait_send()


def per_device(n_box, n_dir, leaf_patterns, occupancy, pair_lists):
    _, count, _, lt, lp = leaf_patterns.shape
    assert leaf_patterns.shape[0] == 2
    slab = 2 * lt // n_dir
    bf16 = jnp.bfloat16
    first_high, first_low = halves(interp_table(lp, 0.0).T)
    c1 = np.concatenate([first_high, first_high, first_low], axis=0)
    row_high, row_low = halves(interp_table(lt, 0.5))
    r1 = np.concatenate([row_high, row_high, row_low], axis=1)
    row_high, row_low = halves(interp_table(2 * lt, 0.5).reshape(2, 2 * lt, 2 * lt))
    r2 = np.concatenate([row_high, row_high, row_low], axis=2)
    high, low = halves(interp_table(2 * lp, 0.0).T)
    c2 = np.concatenate([high, high, low], axis=0)
    st, _, cp, _ = sines(2 * lt, 2 * lp)
    angle = phase_first * st[:, None] * cp[None]
    ph1 = np.stack([np.cos(angle), np.sin(angle)]).astype(np.float32)
    st, ct, cp, sp = sines(4 * lt, 4 * lp)
    angle = phase_second * st[:, None] * sp[None]
    ph2 = np.stack([np.cos(angle), np.sin(angle)]).astype(np.float32)
    polar = np.stack([st, ct])[:, :, None].astype(np.float32)
    azim = np.stack([cp, sp]).astype(np.float32)
    series = series_table(n_box // 2)
    operands = (
        leaf_patterns, occupancy, pair_lists, series, c1, r1, r2, c2, ph1, ph2, polar, azim
    )
    chunk = (2, slab, 4 * lp)
    f32 = jnp.float32
    rows = 2 * lt
    result = pl.pallas_call(
        functools.partial(kernel, (n_box, n_dir, count, lt, lp, slab)),
        out_shape=jax.ShapeDtypeStruct((n_dir, count) + chunk, f32),
        in_specs=[pl.BlockSpec(memory_space=pltpu.HBM)] * len(operands),
        out_specs=pl.BlockSpec(memory_space=pltpu.VMEM),
        scratch_shapes=[
            pltpu.VMEM(leaf_patterns.shape, f32),
            pltpu.SMEM(occupancy.shape, jnp.int32),
            pltpu.SMEM(pair_lists.shape, jnp.int32),
            pltpu.SMEM(series.shape, f32),
            pltpu.VMEM(c1.shape, bf16),
            pltpu.VMEM(r1.shape, bf16),
            pltpu.VMEM(r2.shape[1:], bf16),
            pltpu.VMEM(c2.shape, bf16),
            pltpu.VMEM(ph1.shape, f32),
            pltpu.VMEM((2, rows, 4 * lp), f32),
            pltpu.VMEM((2, rows, 1), f32),
            pltpu.VMEM(azim.shape, f32),
            pltpu.VMEM((count, 4, lt, lp), f32),
            pltpu.VMEM((2, count, 2, 4, lt, lp), f32),
            pltpu.VMEM((4 * lt, 3 * lp), bf16),
            pltpu.VMEM((3 * lt, 8 * lp), bf16),
            pltpu.VMEM((2, rows, 2 * lp), f32),
            pltpu.VMEM((6 * lt, 8 * lp), bf16),
            pltpu.VMEM((8 * lt, 6 * lp), bf16),
            pltpu.VMEM((count, n_dir) + chunk, f32),
            pltpu.VMEM((2, 2, rows, 4 * lp), f32),
            pltpu.SemaphoreType.DMA((len(operands),)),
            pltpu.SemaphoreType.DMA((2, count, 2)),
            pltpu.SemaphoreType.DMA((2, count, 2)),
            pltpu.SemaphoreType.DMA((count, n_dir)),
            pltpu.SemaphoreType.DMA((count, n_dir)),
        ],
        compiler_params=pltpu.CompilerParams(
            collective_id=0, has_side_effects=True, vmem_limit_bytes=64500000
        ),
    )(*[jnp.asarray(operand) for operand in operands])
    return result.reshape(1, 1, n_dir * count, *chunk)


def solution(mesh):
    placed = (P("box", "dir", None, None, None), P("box"), P())
    return jax.shard_map(
        functools.partial(per_device, mesh.shape["box"], mesh.shape["dir"]),
        mesh=mesh,
        in_specs=placed,
        out_specs=P("box", None, None, None, "dir", None),
        check_vma=False,
    )
```

time: 72.7 us -> 50.1 us (0.69)
  the two profiles are of different devices: /device:TPU:1 before, /device:TPU:21 now
where the time goes in v1:
time: 50.1 us; the launch traced here: 49.9 us
  Pallas kernels  46.7 us (93%)
  local copies, waits for them, and re-layouts  3.19 us (6%)
    pallas_call x1, Pallas kernels, per_device(): pl.pallas_call(functools.partial(kernel, (n_box, n_dir, count, lt, lp, sl...  46.7 us
    unnamed x1, local copies, waits for them, and re-layouts  3.19 us

profile of v1, /device:TPU:21, one launch (start us, length us, event | category | flops | bytes accessed | tf_op | source)
XLA Modules:
  0.0 49.9 jit_solution(11433517201335712557)
XLA Ops:
  0.0 46.7 %shard_map.118 = f32[4,4,2,32,512]{4,3,2,1,0:T(8,128)} custom-call(f32[2,4,2,64,128]{4,3,2,1,0:T(8,128)} %leaf_in.1, s32[2]{0:T(128)} %occ_in.1, s32[4,1,4]{2,1,0:T(1,128)} %lists_in.1, f32[4,74]{1,0:T(4,128)} %constant.18.clone.series_in, bf16[384,256]{1,0:T(8,128)(2,1)} %constant.19.clone.c1_in, bf16[128,192]{1,0:T(8,128)(2,1)} %constant.20.clone.r1_in, ...), custom_call_target="tpu_custom_call" | custom-call | tf_op jit(solution)/shard_map/pallas_call | solution.py:326
  46.7 3.2 %copy.14 = f32[1,1,16,2,32,512]{5,4,3,2,1,0:T(8,128)} copy(f32[1,1,16,2,32,512]{5,4,3,2,1,0:T(8,128)} %bitcast.1) | data formatting | bytes 4194304

commit v2 on v1

--- a/solution.py
+++ b/solution.py
@@ -78,7 +78,7 @@
     polar_in, azim_in,
     out,
     leaf, occ, lists, series, c1, r1, r2, c2, ph1, ph2, polar, azim,
-    mine, taken, lhs1, rhs1, first, rhs2, lhs2, ready, oper,
+    mine, taken, lhs1, rhs1, first, rhs2, lhs2, wide, ready, oper,
     loads, ls, lr, ds, dr,
 ):
     n_box, n_dir, count, lt, lp, slab = sizes
@@ -215,9 +215,9 @@
             lhs1[rows, 0:lp] = high
             lhs1[rows, lp : 2 * lp] = low
             lhs1[rows, 2 * lp : 3 * lp] = high
-        wide = dot(lhs1[...], c1[...])
+        stretched = dot(lhs1[...], c1[...])
         for k in range(4):
-            high, low = split(wide[k * lt : (k + 1) * lt])
+            high, low = split(stretched[k * lt : (k + 1) * lt])
             columns = pl.ds(k * 2 * lp, 2 * lp)
             rhs1[0:lt, columns] = high
             rhs1[lt : 2 * lt, columns] = low
@@ -251,10 +251,9 @@
             lhs2[rows, 0 : 2 * lp] = high
             lhs2[rows, 2 * lp : 4 * lp] = low
             lhs2[rows, 4 * lp : 6 * lp] = high
+        wide[...] = dot(lhs2[...], c2[...])
         for d in range(n_dir):
-            sr, si, dre, dim = [
-                dot(lhs2[pl.ds(k * 2 * lt + d * slab, slab), :], c2[...]) for k in range(4)
-            ]
+            sr, si, dre, dim = [wide[pl.ds(k * 2 * lt + d * slab, slab), :] for k in range(4)]
             rows = pl.ds(d * slab, slab)
             cosine, sine = ph2[0, rows], ph2[1, rows]
             gr = cosine * sr - sine * dim
@@ -348,6 +347,7 @@
             pltpu.VMEM((2, rows, 2 * lp), f32),
             pltpu.VMEM((6 * lt, 8 * lp), bf16),
             pltpu.VMEM((8 * lt, 6 * lp), bf16),
+            pltpu.VMEM((8 * lt, 4 * lp), f32),
             pltpu.VMEM((count, n_dir) + chunk, f32),
             pltpu.VMEM((2, 2, rows, 4 * lp), f32),
             pltpu.SemaphoreType.DMA((len(operands),)),

time: 50.1 us -> 42.6 us (0.85)
  Pallas kernels: 46.7 us -> 39.3 us
    pallas_call x1, Pallas kernels: 46.7 us -> 39.3 us  [per_device(): pl.pallas_call(functools.partial(kernel, (n_box, n_dir, count, lt, lp, sl...]
where the time goes in v2:
time: 42.6 us; the launch traced here: 42.5 us
  Pallas kernels  39.3 us (92%)
  local copies, waits for them, and re-layouts  3.19 us (7%)
    pallas_call x1, Pallas kernels, per_device(): pl.pallas_call(functools.partial(kernel, (n_box, n_dir, count, lt, lp, sl...  39.3 us
    unnamed x1, local copies, waits for them, and re-layouts  3.19 us

profile of v2, /device:TPU:21, one launch (start us, length us, event | category | flops | bytes accessed | tf_op | source)
XLA Modules:
  0.0 42.5 jit_solution(13727696485001222270)
XLA Ops:
  0.0 39.3 %shard_map.118 = f32[4,4,2,32,512]{4,3,2,1,0:T(8,128)} custom-call(f32[2,4,2,64,128]{4,3,2,1,0:T(8,128)} %leaf_in.1, s32[2]{0:T(128)} %occ_in.1, s32[4,1,4]{2,1,0:T(1,128)} %lists_in.1, f32[4,74]{1,0:T(4,128)} %constant.18.clone.series_in, bf16[384,256]{1,0:T(8,128)(2,1)} %constant.19.clone.c1_in, bf16[128,192]{1,0:T(8,128)(2,1)} %constant.20.clone.r1_in, ...), custom_call_target="tpu_custom_call" | custom-call | tf_op jit(solution)/shard_map/pallas_call | solution.py:325
  39.3 3.2 %copy.14 = f32[1,1,16,2,32,512]{5,4,3,2,1,0:T(8,128)} copy(f32[1,1,16,2,32,512]{5,4,3,2,1,0:T(8,128)} %bitcast.1) | data formatting | bytes 4194304

commit v3 on v2

--- a/solution.py
+++ b/solution.py
@@ -357,9 +357,9 @@
             pltpu.SemaphoreType.DMA((count, n_dir)),
         ],
         compiler_params=pltpu.CompilerParams(
-            collective_id=0, has_side_effects=True, vmem_limit_bytes=64500000
+            collective_id=0, has_side_effects=True, vmem_limit_bytes=48 << 20
         ),
-    )(*[jnp.asarray(operand) for operand in operands])
+    )(*[pltpu.with_memory_space_constraint(jnp.asarray(operand), pltpu.HBM) for operand in operands])
     return result.reshape(1, 1, n_dir * count, *chunk)
 
 

time: 42.6 us -> 39.4 us (0.925)
  local copies, waits for them, and re-layouts: 3.19 us -> 1.32 us
  Pallas kernels: 39.3 us -> 37.9 us
    unnamed x1, local copies, waits for them, and re-layouts: 3.19 us -> 1.32 us
    pallas_call x1, Pallas kernels: 39.3 us -> 37.9 us  [per_device(): pl.pallas_call(functools.partial(kernel, (n_box, n_dir, count, lt, lp, sl...]
where the time goes in v3:
time: 39.4 us; the launch traced here: 39.2 us
  Pallas kernels  37.9 us (96%)
  local copies, waits for them, and re-layouts  1.32 us (3%)
    pallas_call x1, Pallas kernels, per_device(): pl.pallas_call(functools.partial(kernel, (n_box, n_dir, count, lt, lp, sl...  37.9 us
    unnamed x1, local copies, waits for them, and re-layouts  1.32 us

profile of v3, /device:TPU:21, one launch (start us, length us, event | category | flops | bytes accessed | tf_op | source)
XLA Modules:
  0.0 39.2 jit_solution(13805595001194786775)
XLA Ops:
  0.0 37.9 %shard_map.118 = f32[4,4,2,32,512]{4,3,2,1,0:T(8,128)S(1)} custom-call(f32[2,4,2,64,128]{4,3,2,1,0:T(8,128)} %leaf_in.1, s32[2]{0:T(128)} %occ_in.1, s32[4,1,4]{2,1,0:T(1,128)} %lists_in.1, f32[4,74]{1,0:T(4,128)} %constant.18.clone.series_in, bf16[384,256]{1,0:T(8,128)(2,1)} %constant.19.clone.c1_in, bf16[128,192]{1,0:T(8,128)(2,1)} %constant.20.clone.r1_in, ...), custom_call_target="tpu_custom_call" | custom-call | tf_op jit(solution)/shard_map/pallas_call | solution.py:325
  37.9 1.3 %copy.14 = f32[1,1,16,2,32,512]{5,4,3,2,1,0:T(8,128)} copy(f32[1,1,16,2,32,512]{5,4,3,2,1,0:T(8,128)S(1)} %bitcast.1) | data formatting | bytes 4194304

commit v4 on v3

--- a/solution.py
+++ b/solution.py
@@ -230,7 +230,7 @@
 
     sign = (2 * half - 1).astype(jnp.float32)
 
-    def add_side(r, side):
+    def add_side(r, side, closing):
         for place in range(2):
             l_copy(r, side, place).wait_recv()
             fr, fi = first_level(taken.at[side, r, place])
@@ -252,28 +252,36 @@
             lhs2[rows, 2 * lp : 4 * lp] = low
             lhs2[rows, 4 * lp : 6 * lp] = high
         wide[...] = dot(lhs2[...], c2[...])
-        for d in range(n_dir):
-            sr, si, dre, dim = [wide[pl.ds(k * 2 * lt + d * slab, slab), :] for k in range(4)]
-            rows = pl.ds(d * slab, slab)
+        for o in range(1, n_dir + 1):
+            d = (me + o) % n_dir
+            offset = pl.multiple_of(d * slab, slab)
+            sr, si, dre, dim = [
+                wide[pl.ds(k * 2 * lt + offset, slab), :] for k in range(4)
+            ]
+            rows = pl.ds(offset, slab)
             cosine, sine = ph2[0, rows], ph2[1, rows]
             gr = cosine * sr - sine * dim
             gi = cosine * si + sine * dre
             pr, pi = oper[side, 0, rows], oper[side, 1, rows]
             ready[r, d, 0] += pr * gr - pi * gi
             ready[r, d, 1] += pr * gi + pi * gr
+            if o < n_dir:
+                @pl.when(closing)
+                def _():
+                    d_copy(r, o).start()
 
     def level_step(q, carry):
         r = q // 2
         side = q % 2
 
+        closing = jnp.logical_or(side == 1, jnp.logical_not(has_upper))
+
         @pl.when(jnp.where(side == 0, has_lower, has_upper))
         def _():
-            add_side(r, side)
+            add_side(r, side, closing)
 
         @pl.when(side == 1)
         def _():
-            for o in range(1, n_dir):
-                d_copy(r, o).start()
             out[me, r] = ready[r, me]
 
         return carry

time: 39.4 us -> 39.3 us (level)
  no operation moved by 1% of the time
where the time goes in v4:
time: 39.3 us; the launch traced here: 39.1 us
  Pallas kernels  37.8 us (96%)
  local copies, waits for them, and re-layouts  1.32 us (3%)
    pallas_call x1, Pallas kernels, per_device(): pl.pallas_call(functools.partial(kernel, (n_box, n_dir, count, lt, lp, sl...  37.8 us
    unnamed x1, local copies, waits for them, and re-layouts  1.32 us

profile of v4, /device:TPU:21, one launch (start us, length us, event | category | flops | bytes accessed | tf_op | source)
XLA Modules:
  0.0 39.1 jit_solution(2008596189066277579)
XLA Ops:
  0.0 37.8 %shard_map.118 = f32[4,4,2,32,512]{4,3,2,1,0:T(8,128)S(1)} custom-call(f32[2,4,2,64,128]{4,3,2,1,0:T(8,128)} %leaf_in.1, s32[2]{0:T(128)} %occ_in.1, s32[4,1,4]{2,1,0:T(1,128)} %lists_in.1, f32[4,74]{1,0:T(4,128)} %constant.18.clone.series_in, bf16[384,256]{1,0:T(8,128)(2,1)} %constant.19.clone.c1_in, bf16[128,192]{1,0:T(8,128)(2,1)} %constant.20.clone.r1_in, ...), custom_call_target="tpu_custom_call" | custom-call | tf_op jit(solution)/shard_map/pallas_call | solution.py:333
  37.8 1.3 %copy.14 = f32[1,1,16,2,32,512]{5,4,3,2,1,0:T(8,128)} copy(f32[1,1,16,2,32,512]{5,4,3,2,1,0:T(8,128)S(1)} %bitcast.1) | data formatting | bytes 4194304
